TPU v7x, 32 devices: a whole 2x2x4 slice. The times are simulated.
32 devices in a mesh: groups: 2 (over y), seq: 4 (over x, core), tensor: 4 (over z).
Axes of the slice: x: 2, y: 2, z: 4, core: 2. Of those that a mesh axis runs over, the one named last changes fastest.
Arguments:
- patches: bfloat16 [2056, 1280], P(('groups', 'seq')), parts along dimension 0, may hold values from -6 to 6
- latents: bfloat16 [64, 1280], replicated, may hold values from -160 to 160
- wq_res: bfloat16 [1280, 1536], P(None, 'tensor'), may hold values from -0.15625 to 0.15625
- wk_res: bfloat16 [1280, 1536], P(None, 'tensor'), may hold values from -0.3125 to 0.3125
- wv_res: bfloat16 [1280, 1536], P(None, 'tensor'), may hold values from -0.15625 to 0.15625
- wo_res: bfloat16 [1536, 1280], P('tensor'), may hold values from -0.625 to 0.625
- text: bfloat16 [3072, 8192], P('groups', 'seq'), parts along dimension 0, may hold values from -240 to 240
- norm_gain: bfloat16 [8192], P('seq'), may hold values from 0.25 to 1.75
- wq_x: bfloat16 [8192, 8192], P('seq', 'tensor'), may hold values from -0.0625 to 0.0625
- wk_x: bfloat16 [1280, 8192], P(None, 'tensor'), may hold values from -0.15625 to 0.15625
- wv_x: bfloat16 [1280, 8192], P(None, 'tensor'), may hold values from -0.15625 to 0.15625
- wo_x: bfloat16 [8192, 8192], P('tensor', 'seq'), may hold values from -0.25 to 0.25
- gate_x: float32 [8192], P('seq'), may hold values from -1.5 to 1.5
- text_image: int32 [3072], P('groups'), parts along dimension 0, may hold values from -1 to 3, as said below
Outputs:
- text_out: float32 [3072, 8192], P('groups', 'seq'), parts along dimension 0
- page_latents: bfloat16 [512, 1280], P(('groups', 'seq')), parts along dimension 0
There are 2 independent parts, one for each index of `groups`. A program takes and returns all parts, laid end to end along the dimension named above; an argument that names none is the same for every part. Nothing has to cross between parts.
Inputs may be any that keep to these rules, and one draw needn't show every extreme that they name: text_image[t] is the index of the last image placed at or before token t, -1 before the first image; it never falls along the tokens, and every one of the 4 images is the value of some tokens.
All inputs are finite; a program needn't handle non-finite values.
Results may differ from a plain program's by a relative error of at most 0.015.
The roundings to bfloat16 on the way count: a program that leaves them out, or rounds other values in their place, can miss the bound.
Values may be sent and summed in bfloat16 or wider, within the bound.
A program may use at most 192 MiB of HBM per device.

v0:
```python
import math
import jax
import jax.numpy as jnp
from jax import lax
from jax.sharding import PartitionSpec as P

WIDTH = 8192
HEAD = 128
RES_HEAD = 96
PATCH_IMG = 257


def shards(
    patches,
    latents,
    wq_res,
    wk_res,
    wv_res,
    wo_res,
    text,
    norm_gain,
    wq_x,
    wk_x,
    wv_x,
    wo_x,
    gate_x,
    text_image,
):
    inv_res = 1.0 / math.sqrt(RES_HEAD)
    inv_root = 1.0 / math.sqrt(HEAD)
    lat_count = latents.shape[0]
    img_count = patches.shape[0] // PATCH_IMG
    heads_res = wq_res.shape[1] // RES_HEAD
    queries = (
        jnp.dot(latents, wq_res, preferred_element_type=jnp.float32)
        .astype(jnp.bfloat16)
        .reshape(lat_count, heads_res, RES_HEAD)
    )
    page_keys = (
        jnp.dot(patches, wk_res, preferred_element_type=jnp.float32)
        .astype(jnp.bfloat16)
        .reshape(img_count, PATCH_IMG, heads_res, RES_HEAD)
    )
    page_values = (
        jnp.dot(patches, wv_res, preferred_element_type=jnp.float32)
        .astype(jnp.bfloat16)
        .reshape(img_count, PATCH_IMG, heads_res, RES_HEAD)
    )
    scores = (
        jnp.einsum("lhd,iphd->ihlp", queries, page_keys, preferred_element_type=jnp.float32)
        * inv_res
    )
    summit = jnp.max(scores, axis=3, keepdims=True)
    weights = jnp.exp(scores - summit).astype(jnp.bfloat16)
    totals = jnp.sum(weights, axis=3, dtype=jnp.float32)
    blended = jnp.einsum(
        "ihlp,iphd->ihld", weights, page_values, preferred_element_type=jnp.float32
    )
    pooled = (
        (blended / totals[:, :, :, None])
        .transpose(0, 2, 1, 3)
        .reshape(img_count * lat_count, heads_res * RES_HEAD)
        .astype(jnp.bfloat16)
    )
    partial_value = jnp.dot(pooled, wo_res, preferred_element_type=jnp.float32)
    latent_sum = lax.psum(partial_value, "tensor")
    repeated = jnp.tile(latents, (img_count, 1)).astype(jnp.float32)
    page_latents = (repeated + latent_sum).astype(jnp.bfloat16)
    tok_count = text.shape[0]
    hidden = text.astype(jnp.float32)
    squares = jnp.sum(hidden * hidden, axis=1)
    scaled = (hidden * norm_gain.astype(jnp.float32)).astype(jnp.bfloat16)
    query_part = jnp.dot(scaled, wq_x, preferred_element_type=jnp.float32)
    squares, query_sum = lax.psum((squares, query_part), "seq")
    inverse = lax.rsqrt(squares / WIDTH + 1e-05)
    heads_x = wq_x.shape[1] // HEAD
    text_queries = (query_sum * inverse[:, None]).astype(jnp.bfloat16)
    own_keys = jnp.dot(page_latents, wk_x, preferred_element_type=jnp.float32).astype(jnp.bfloat16)
    own_values = jnp.dot(page_latents, wv_x, preferred_element_type=jnp.float32).astype(
        jnp.bfloat16
    )
    cross_keys, cross_values = (
        lax.all_gather(own_keys, "seq", axis=0, tiled=True),
        lax.all_gather(own_values, "seq", axis=0, tiled=True),
    )
    lat_all = cross_keys.shape[0]
    cross_keys = cross_keys.reshape(lat_all, heads_x, HEAD)
    cross_values = cross_values.reshape(lat_all, heads_x, HEAD)
    latent_owner = jnp.arange(lat_all, dtype=jnp.int32) // lat_count
    row_block = math.gcd(tok_count, 512)
    n_blocks = tok_count // row_block
    q_blocks = text_queries.reshape(n_blocks, row_block, heads_x, HEAD)
    img_blocks = text_image.reshape(n_blocks, row_block)

    def attend(inputs):
        q_rows, img_rows = inputs
        logits = (
            jnp.einsum("thd,lhd->htl", q_rows, cross_keys, preferred_element_type=jnp.float32)
            * inv_root
        )
        allowed = img_rows[:, None] == latent_owner[None, :]
        logits = jnp.where(allowed[None, :, :], logits, -1e30)
        row_peak = jnp.max(logits, axis=2, keepdims=True)
        probs_bf = jnp.exp(logits - row_peak).astype(jnp.bfloat16)
        row_total = jnp.sum(probs_bf, axis=2, dtype=jnp.float32)
        mixture = jnp.einsum(
            "htl,lhd->thd", probs_bf, cross_values, preferred_element_type=jnp.float32
        )
        visible = (img_rows >= 0).astype(jnp.float32)
        return (mixture / row_total.T[:, :, None] * visible[:, None, None]).astype(jnp.bfloat16)

    attended = lax.map(attend, (q_blocks, img_blocks)).reshape(tok_count, heads_x * HEAD)
    block_part = jnp.dot(attended, wo_x, preferred_element_type=jnp.float32)
    gate_open = jnp.tanh(gate_x)
    block_whole = lax.psum(block_part.astype(jnp.bfloat16), "tensor").astype(jnp.float32)
    text_out = hidden + gate_open * block_whole
    return (text_out, page_latents)


def solution(mesh):
    in_specs = (
        P(("groups", "seq"), None),
        P(),
        P(None, "tensor"),
        P(None, "tensor"),
        P(None, "tensor"),
        P("tensor", None),
        P("groups", "seq"),
        P("seq"),
        P("seq", "tensor"),
        P(None, "tensor"),
        P(None, "tensor"),
        P("tensor", "seq"),
        P("seq"),
        P("groups"),
    )
    out_specs = (P("groups", "seq"), P(("groups", "seq"), None))
    return jax.shard_map(shards, mesh=mesh, in_specs=in_specs, out_specs=out_specs, check_vma=False)
```

profile of v0, /device:TPU:0, one launch (start us, length us, event | category | flops | bytes accessed | tf_op | source)
XLA Modules:
  0.0 635.0 jit_solution(5875707518718355605)
XLA Ops:
  16.7 39.3 %all-reduce.6.cloned.1.call-done = f32[64,1280]{1,0:T(8,128)} async-done(((f32[64,1280]{1,0:T(8,128)}), f32[64,1280]{1,0:T(8,128)}) %all-reduce.6.cloned.1.call-update) | async-done | bytes 327696 | tf_op jit(solution)/shard_map/psum | solution.py:66
  56.9 4.3 convolution_convert_fusion.1
  61.3 4.2 convolution_convert_fusion.2
  65.6 19.3 %fusion.12 = f32[1536,2048]{1,0:T(8,128)} fusion(bf16[2048,2048]{1,0:T(8,128)(2,1)} %param.24, bf16[1536,2048]{1,0:T(8,128)(2,1)} %param.22, f32[2048]{0:T(1024)S(1)} %convert_element_type.74), kind=kOutput, calls=%fused_computation.30 | convolution fusion | flops 12894339072 | bytes 27271168 | tf_op jit(solution)/shard_map/dot_general | solution.py:73
  85.6 4.3 fusion.10
  89.9 6.4 %psum.29 = f32[1536]{0:T(1024)S(1)} all-reduce(f32[1536]{0:T(1024)S(1)} %fusion.10), channel_id=1, replica_groups=mesh['groups'=2,'seq'=4,'tensor'=4] {'seq'}, use_global_device_ids=true, to_apply=%region_2.0 | all-reduce | flops 1536 | bytes 12288 | tf_op jit(solution)/shard_map/psum | solution.py:74
  99.3 220.7 %all-reduce.4.cloned.1.call-done = f32[1536,2048]{1,0:T(8,128)} async-done(((f32[1536,2048]{1,0:T(8,128)}), f32[1536,2048]{1,0:T(8,128)}) %all-reduce.4.cloned.1.call-update) | async-done | bytes 12582928 | tf_op jit(solution)/shard_map/psum | solution.py:74
  320.0 8.4 %fusion.11 = bf16[192,8,16,128]{3,1,2,0:T(8,128)(2,1)} fusion(f32[1536,2048]{1,0:T(8,128)} %all-reduce.4.cloned.1.call-done, f32[1536]{0:T(1024)S(1)} %add_rsqrt_fusion), kind=kLoop, calls=%fused_computation.29 | loop fusion | flops 6291456 | bytes 18880512
  328.4 7.8 %copy.38 = bf16[192,8,16,128]{3,2,1,0:T(8,128)(2,1)} copy(bf16[192,8,16,128]{3,1,2,0:T(8,128)(2,1)} %fusion.11) | data formatting | bytes 12582912
  336.1 37.6 %while.11 = (s32[]{:T(128)}, bf16[3,512,16,128]{3,2,1,0:T(8,128)(2,1)}, s32[3,512]{1,0:T(4,128)S(1)}, bf16[3,512,16,128]{3,2,1,0:T(8,128)(2,1)}, bf16[256,16,128...) while((s32[]{:T(128)}, bf16[3,512,16,128]{3,2,1,0:T(8,128)(2,1)}, ...), condition=%wide.region_9.10_spmd.clone, body=%wide.region_6.9_spmd.clone.sunk | while | flops 1104268288 | bytes 40548948 | solution.py:112
  336.3 2.0 constant_dynamic-slice_fusion.5
  338.3 2.4 fusion.50
  342.5 3.5 fusion.51
  346.0 2.7 copy_dynamic-update-slice_fusion.2
  348.9 2.0 constant_dynamic-slice_fusion.5
  350.8 2.4 fusion.50
  355.1 3.5 fusion.51
  358.5 2.7 copy_dynamic-update-slice_fusion.2
  363.3 2.4 fusion.50
  367.6 3.5 fusion.51
  371.0 2.7 copy_dynamic-update-slice_fusion.2
  373.8 18.9 %convolution_convert_fusion = bf16[1536,2048]{1,0:T(8,128)(2,1)} fusion(bf16[2048,2048]{1,0:T(8,128)(2,1)} %param.27, bf16[192,8,16,128]{3,2,1,0:T(8,128)(2,1)} %bitcast.20), kind=kOutput, calls=%fused_computation.28 | convolution fusion | flops 12888047616 | bytes 20971520 | tf_op jit(solution)/shard_map/dot_general | solution.py:113
  393.3 222.5 %all-reduce.8.cloned.1.call-done = bf16[1536,2048]{1,0:T(8,128)(2,1)} async-done(((bf16[1536,2048]{1,0:T(8,128)(2,1)}), bf16[1536,2048]{1,0:T(8,128)(2,1)}) %all-reduce.8.cloned.1.call-update) | async-done | bytes 6291472 | tf_op jit(solution)/shard_map/psum | solution.py:115
  615.9 12.6 %convert_add_fusion = f32[1536,2048]{1,0:T(8,128)} fusion(bf16[1536,2048]{1,0:T(8,128)(2,1)} %param.22, bf16[1536,2048]{1,0:T(8,128)(2,1)} %all-reduce.8.cloned.1.call-done, f32[2048]{0:T(1024)S(1)} %tanh.3), kind=kLoop, calls=%fused_computation.22 | loop fusion | flops 12582912 | bytes 25174016 | tf_op jit(solution)/shard_map/add | solution.py:116
  (64 shorter events, 22.8 us)
Async XLA Ops:
  7.2 1.5 copy-start
  7.2 48.7 %copy-start.4 = (bf16[64,1280]{1,0:T(8,128)(2,1)S(1)}, bf16[64,1280]{1,0:T(8,128)(2,1)}, u32[]{:S(2)}) copy-start(bf16[64,1280]{1,0:T(8,128)(2,1)} %param.17) | copy-start | bytes 491524
  7.2 8.4 %copy-start.3 = (bf16[384,1280]{1,0:T(8,128)(2,1)S(1)}, bf16[384,1280]{1,0:T(8,128)(2,1)}, u32[]{:S(2)}) copy-start(bf16[384,1280]{1,0:T(8,128)(2,1)} %param.21) | copy-start | bytes 2949124
  7.2 48.7 %all-reduce.6.cloned.1.call-start = ((), (), s32[]{:S(2)}) async-start(), calls=%async_computation.1 | async-start | bytes 655360 | tf_op jit(solution)/shard_map/psum | solution.py:66
  12.3 49.0 %copy-start.7 = (bf16[2048]{0:T(1024)(128)(2,1)S(1)}, bf16[2048]{0:T(1024)(128)(2,1)}, u32[]{:S(2)}) copy-start(bf16[2048]{0:T(1024)(128)(2,1)} %param.23) | copy-start | bytes 12292
  16.6 79.7 %all-gather.5.cloned.1.call-start = ((), (), s32[]{:S(2)}) async-start(), calls=%async_computation.3 | async-start | bytes 1310720 | tf_op jit(solution)/shard_map/all_gather | solution.py:84
  56.9 27.9 %copy-start.2 = (bf16[64,1280]{1,0:T(8,128)(2,1)}, bf16[64,1280]{1,0:T(8,128)(2,1)S(1)}, u32[]{:S(2)}) copy-start(bf16[64,1280]{1,0:T(8,128)(2,1)S(1)} %add_convert_fusion) | copy-start | bytes 491524
  61.2 36.6 %all-gather.3.cloned.1.call-start = ((), (), s32[]{:S(2)}) async-start(), calls=%async_computation.2 | async-start | bytes 1310720 | tf_op jit(solution)/shard_map/all_gather | solution.py:83
  65.5 254.5 %all-reduce.4.cloned.1.call-start = ((), (), s32[]{:S(2)}) async-start(), calls=%async_computation | async-start | bytes 25165824 | tf_op jit(solution)/shard_map/psum | solution.py:74
  84.9 0.7 copy-start.5
  84.9 531.0 %all-reduce.8.cloned.1.call-start = ((), (), s32[]{:S(2)}) async-start(), calls=%async_computation.4 | async-start | bytes 12582912 | tf_op jit(solution)/shard_map/psum | solution.py:115
  392.6 0.7 copy-start.6
  615.9 12.6 %copy-start.1 = (bf16[1280,384]{1,0:T(8,128)(2,1)S(1)}, bf16[1280,384]{1,0:T(8,128)(2,1)}, u32[]{:S(2)}) copy-start(bf16[1280,384]{1,0:T(8,128)(2,1)} %param.19) | copy-start | bytes 2949124
Sparse Core Ops, SparseCore 0:
  16.7 39.1 all-reduce.5
  61.4 16.4 all-gather.4
  79.4 16.8 all-gather.2
  99.2 220.7 all-reduce.3
  392.8 223.0 all-reduce.7
where the time goes:
time: 636 us; the launch traced here: 635 us
  waiting for transfers between devices  483 us (76%)
  matrix products  70.9 us (11%)
  other arithmetic  32.4 us (5%)
  local copies, waits for them, and re-layouts  28.4 us (4%)
  between operations  14 us (2%)
  blocking collectives  6.37 us (1%)
    psum x1, waiting for transfers between devices, shards(): lax.psum(block_part.astype(jnp.bfloat16), 'tensor').astype(jnp.float32)  223 us
    psum x1, waiting for transfers between devices, shards(): squares, query_sum = lax.psum((squares, query_part), 'seq')  221 us
    psum x1, waiting for transfers between devices, shards(): latent_sum = lax.psum(partial_value, 'tensor')  39.3 us
    dot_general x1, matrix products, shards(): query_part = jnp.dot(scaled, wq_x, preferred_element_type=jnp.float32)  19.3 us
    dot_general x1, matrix products, shards(): block_part = jnp.dot(attended, wo_x, preferred_element_type=jnp.float32)  18.9 us
    unnamed x19, local copies, waits for them, and re-layouts  13.5 us
  transfers between devices with their start and end apart: 5, of which 3 were waited for; matrix products, arithmetic and copies ran while one was open for 5% of the time, Pallas kernels for 0%

commit v1 on v0

--- a/solution.py
+++ b/solution.py
@@ -8,6 +8,18 @@
 HEAD = 128
 RES_HEAD = 96
 PATCH_IMG = 257
+
+
+def prepare_matrix_in(base_x):
+    link_axis = "tensor"
+    num = lax.axis_size(link_axis)
+    long_array = base_x
+    for kk in [nth for nth in (1, 2, 4, 8, 16) if nth < num]:
+        arrivals = []
+        for m in range(num):
+            arrivals.append((m, m ^ kk))
+        long_array = long_array + lax.ppermute(long_array, link_axis, arrivals)
+    return long_array
 
 
 def shards(
@@ -63,7 +75,7 @@
         .astype(jnp.bfloat16)
     )
     partial_value = jnp.dot(pooled, wo_res, preferred_element_type=jnp.float32)
-    latent_sum = lax.psum(partial_value, "tensor")
+    latent_sum = prepare_matrix_in(partial_value)
     repeated = jnp.tile(latents, (img_count, 1)).astype(jnp.float32)
     page_latents = (repeated + latent_sum).astype(jnp.bfloat16)
     tok_count = text.shape[0]

time: 636 us -> 624 us (0.981)
  waiting for transfers between devices: 483 us -> 466 us
    psum x1 -> x0, waiting for transfers between devices: 39.3 us -> none  [shards(): latent_sum = lax.psum(partial_value, 'tensor')]
    ppermute x0 -> x2, waiting for transfers between devices: none -> 21.8 us  [prepare_matrix_in(): long_array = long_array + lax.ppermute(long_array, link_axis, arrivals)]
  transfers between devices with their start and end apart: 5 -> 6, of which waited for: 3 -> 4; matrix products, arithmetic and copies ran while one was open for 5% -> 5% of each run, Pallas kernels for 0% -> 0%
where the time goes in v1:
time: 624 us; the launch traced here: 623 us
  waiting for transfers between devices  466 us (75%)
  matrix products  69.9 us (11%)
  other arithmetic  31.4 us (5%)
  local copies, waits for them, and re-layouts  28.4 us (5%)
  between operations  14 us (2%)
  blocking collectives  6.62 us (1%)
    psum x1, waiting for transfers between devices, shards(): lax.psum(block_part.astype(jnp.bfloat16), 'tensor').astype(jnp.float32)  223 us
    psum x1, waiting for transfers between devices, shards(): squares, query_sum = lax.psum((squares, query_part), 'seq')  222 us
    ppermute x2, waiting for transfers between devices, prepare_matrix_in(): long_array = long_array + lax.ppermute(long_array, link_axis, arrivals)  21.8 us
    dot_general x1, matrix products, shards(): query_part = jnp.dot(scaled, wq_x, preferred_element_type=jnp.float32)  19 us
    dot_general x1, matrix products, shards(): block_part = jnp.dot(attended, wo_x, preferred_element_type=jnp.float32)  18.9 us
    unnamed x19, local copies, waits for them, and re-layouts  13.5 us
    add x1, other arithmetic, shards(): text_out = hidden + gate_open * block_whole  12.6 us
  transfers between devices with their start and end apart: 6, of which 4 were waited for; matrix products, arithmetic and copies ran while one was open for 5% of the time, Pallas kernels for 0%

profile of v1, /device:TPU:0, one launch (start us, length us, event | category | flops | bytes accessed | tf_op | source)
XLA Modules:
  0.0 623.0 jit_solution(2080105175972817407)
XLA Ops:
  15.8 3.1 collective-permute-start
  19.0 7.7 %collective-permute-done = f32[64,1280]{1,0:T(8,128)S(1)} collective-permute-done((f32[64,1280]{1,0:T(8,128)S(1)}, f32[64,1280]{1,0:T(8,128)S(1)}, u32[]{:S(2)}, u32[]{:S(2)}) %collective-permute-start) | collective-permute-done | bytes 327712 | tf_op jit(solution)/shard_map/ppermute | solution.py:21
  26.7 2.8 collective-permute-start.1
  29.5 14.0 %collective-permute-done.1 = f32[64,1280]{1,0:T(8,128)S(1)} collective-permute-done((f32[64,1280]{1,0:T(8,128)S(1)}, f32[64,1280]{1,0:T(8,128)S(1)}, u32[]{:S(2)}, u32[]{:S(2)}) %collective-permute-start.1) | collective-permute-done | bytes 327712 | tf_op jit(solution)/shard_map/ppermute | solution.py:21
  43.6 4.3 convolution_convert_fusion.1
  48.0 4.2 convolution_convert_fusion.2
  52.3 19.0 %fusion.12 = f32[1536,2048]{1,0:T(8,128)} fusion(bf16[2048,2048]{1,0:T(8,128)(2,1)} %param.24, bf16[1536,2048]{1,0:T(8,128)(2,1)} %param.22, f32[2048]{0:T(1024)S(1)} %convert_element_type.74), kind=kOutput, calls=%fused_computation.30 | convolution fusion | flops 12894339072 | bytes 27271168 | tf_op jit(solution)/shard_map/dot_general | solution.py:85
  72.0 4.3 fusion.10
  76.3 6.6 %psum.22 = f32[1536]{0:T(1024)S(1)} all-reduce(f32[1536]{0:T(1024)S(1)} %fusion.10), channel_id=1, replica_groups=mesh['groups'=2,'seq'=4,'tensor'=4] {'seq'}, use_global_device_ids=true, to_apply=%region_2.0 | all-reduce | flops 1536 | bytes 12288 | tf_op jit(solution)/shard_map/psum | solution.py:86
  86.0 222.0 %all-reduce.3.cloned.1.call-done = f32[1536,2048]{1,0:T(8,128)} async-done(((f32[1536,2048]{1,0:T(8,128)}), f32[1536,2048]{1,0:T(8,128)}) %all-reduce.3.cloned.1.call-update) | async-done | bytes 12582928 | tf_op jit(solution)/shard_map/psum | solution.py:86
  308.0 8.4 %fusion.11 = bf16[192,8,16,128]{3,1,2,0:T(8,128)(2,1)} fusion(f32[1536,2048]{1,0:T(8,128)} %all-reduce.3.cloned.1.call-done, f32[1536]{0:T(1024)S(1)} %add_rsqrt_fusion), kind=kLoop, calls=%fused_computation.29 | loop fusion | flops 6291456 | bytes 18880512
  316.4 7.8 %copy.38 = bf16[192,8,16,128]{3,2,1,0:T(8,128)(2,1)} copy(bf16[192,8,16,128]{3,1,2,0:T(8,128)(2,1)} %fusion.11) | data formatting | bytes 12582912
  324.2 37.6 %while.11 = (s32[]{:T(128)}, bf16[3,512,16,128]{3,2,1,0:T(8,128)(2,1)}, s32[3,512]{1,0:T(4,128)S(1)}, bf16[3,512,16,128]{3,2,1,0:T(8,128)(2,1)}, bf16[256,16,128...) while((s32[]{:T(128)}, bf16[3,512,16,128]{3,2,1,0:T(8,128)(2,1)}, ...), condition=%wide.region_8.9_spmd.clone, body=%wide.region_5.8_spmd.clone.sunk | while | flops 1104268288 | bytes 40548948 | solution.py:124
  326.3 2.4 fusion.50
  330.5 3.5 fusion.51
  334.0 2.7 copy_dynamic-update-slice_fusion.2
  338.8 2.4 fusion.50
  343.1 3.5 fusion.51
  346.5 2.7 copy_dynamic-update-slice_fusion.2
  355.6 3.5 fusion.51
  359.0 2.7 copy_dynamic-update-slice_fusion.2
  361.7 18.9 %convolution_convert_fusion = bf16[1536,2048]{1,0:T(8,128)(2,1)} fusion(bf16[2048,2048]{1,0:T(8,128)(2,1)} %param.27, bf16[192,8,16,128]{3,2,1,0:T(8,128)(2,1)} %bitcast.20), kind=kOutput, calls=%fused_computation.28 | convolution fusion | flops 12888047616 | bytes 20971520 | tf_op jit(solution)/shard_map/dot_general | solution.py:125
  381.3 222.5 %all-reduce.5.cloned.1.call-done = bf16[1536,2048]{1,0:T(8,128)(2,1)} async-done(((bf16[1536,2048]{1,0:T(8,128)(2,1)}), bf16[1536,2048]{1,0:T(8,128)(2,1)}) %all-reduce.5.cloned.1.call-update) | async-done | bytes 6291472 | tf_op jit(solution)/shard_map/psum | solution.py:127
  603.9 12.6 %convert_add_fusion = f32[1536,2048]{1,0:T(8,128)} fusion(bf16[1536,2048]{1,0:T(8,128)(2,1)} %param.22, bf16[1536,2048]{1,0:T(8,128)(2,1)} %all-reduce.5.cloned.1.call-done, f32[2048]{0:T(1024)S(1)} %tanh.3), kind=kLoop, calls=%fused_computation.22 | loop fusion | flops 12582912 | bytes 25174016 | tf_op jit(solution)/shard_map/add | solution.py:128
  (66 shorter events, 27.4 us)
Async XLA Ops:
  7.2 1.5 copy-start
  7.2 36.4 %copy-start.4 = (bf16[64,1280]{1,0:T(8,128)(2,1)S(1)}, bf16[64,1280]{1,0:T(8,128)(2,1)}, u32[]{:S(2)}) copy-start(bf16[64,1280]{1,0:T(8,128)(2,1)} %param.17) | copy-start | bytes 491524
  7.2 8.4 %copy-start.3 = (bf16[384,1280]{1,0:T(8,128)(2,1)S(1)}, bf16[384,1280]{1,0:T(8,128)(2,1)}, u32[]{:S(2)}) copy-start(bf16[384,1280]{1,0:T(8,128)(2,1)} %param.21) | copy-start | bytes 2949124
  7.2 75.8 %all-gather.5.cloned.1.call-start = ((), (), s32[]{:S(2)}) async-start(), calls=%async_computation.2 | async-start | bytes 1310720 | tf_op jit(solution)/shard_map/all_gather | solution.py:96
  14.2 33.8 %copy-start.7 = (bf16[2048]{0:T(1024)(128)(2,1)S(1)}, bf16[2048]{0:T(1024)(128)(2,1)}, u32[]{:S(2)}) copy-start(bf16[2048]{0:T(1024)(128)(2,1)} %param.23) | copy-start | bytes 12292
  15.8 10.8 %collective-permute-start = (f32[64,1280]{1,0:T(8,128)S(1)}, f32[64,1280]{1,0:T(8,128)S(1)}, u32[]{:S(2)}, u32[]{:S(2)}) collective-permute-start(f32[64,1280]{1,0:T(8,128)S(1)} %fusion.25), channel_id=1, source_target_pairs={{0,1},{1,0},{2,3},{3,2},{4,5},{5,4},{6,7},{7,6},{8,9},{9,8},{10,11... | collective-permute-start | bytes 983048 | tf_op jit(solution)/shard_map/ppermute | solution.py:21
  26.7 16.9 %collective-permute-start.1 = (f32[64,1280]{1,0:T(8,128)S(1)}, f32[64,1280]{1,0:T(8,128)S(1)}, u32[]{:S(2)}, u32[]{:S(2)}) collective-permute-start(f32[64,1280]{1,0:T(8,128)S(1)} %add.30), channel_id=1, source_target_pairs={{0,2},{1,3},{2,0},{3,1},{4,6},{5,7},{6,4},{7,5},{8,10},{9,11},{10,... | collective-permute-start | bytes 983048 | tf_op jit(solution)/shard_map/ppermute | solution.py:21
  43.6 27.7 %copy-start.2 = (bf16[64,1280]{1,0:T(8,128)(2,1)}, bf16[64,1280]{1,0:T(8,128)(2,1)S(1)}, u32[]{:S(2)}) copy-start(bf16[64,1280]{1,0:T(8,128)(2,1)S(1)} %add_convert_fusion) | copy-start | bytes 491524
  47.9 36.5 %all-gather.3.cloned.1.call-start = ((), (), s32[]{:S(2)}) async-start(), calls=%async_computation.1 | async-start | bytes 1310720 | tf_op jit(solution)/shard_map/all_gather | solution.py:95
  52.2 255.8 %all-reduce.3.cloned.1.call-start = ((), (), s32[]{:S(2)}) async-start(), calls=%async_computation | async-start | bytes 25165824 | tf_op jit(solution)/shard_map/psum | solution.py:86
  71.3 0.7 copy-start.5
  71.3 532.5 %all-reduce.5.cloned.1.call-start = ((), (), s32[]{:S(2)}) async-start(), calls=%async_computation.3 | async-start | bytes 12582912 | tf_op jit(solution)/shard_map/psum | solution.py:127
  380.6 0.7 copy-start.6
  603.9 12.6 %copy-start.1 = (bf16[1280,384]{1,0:T(8,128)(2,1)S(1)}, bf16[1280,384]{1,0:T(8,128)(2,1)}, u32[]{:S(2)}) copy-start(bf16[1280,384]{1,0:T(8,128)(2,1)} %param.19) | copy-start | bytes 2949124
Sparse Core Ops, SparseCore 0:
  48.1 17.7 all-gather.4
  67.4 16.9 all-gather.2
  87.4 220.5 all-reduce.2
  380.8 223.0 all-reduce.4
